TPU v7x, 32 devices: a whole 2x2x4 slice. The times are simulated.
32 devices in a mesh: segment: 4 (over z), ctx: 4 (over y, x), tp: 2 (over core).
Axes of the slice: x: 2, y: 2, z: 4, core: 2. Of those that a mesh axis runs over, the one named last changes fastest.
Arguments:
- queries: bfloat16 [4, 512, 8, 640], P('segment', 'ctx', 'tp'), may hold values from -200 to 200
- pairs: bfloat16 [4, 512, 8, 256], P('segment', 'ctx', 'tp'), may hold values from -6 to 6
- out_proj: bfloat16 [4, 8, 640, 5120], P('segment', 'tp'), may hold values from -0.625 to 0.625
- lengths: int32 [4, 4], replicated, may hold values from 1 to 256, 512 in all within a row
Outputs:
- scored: bfloat16 [4, 512, 5120], P('segment', 'ctx', 'tp')
Inputs may be any that keep to these rules, and one draw needn't show every extreme that they name: `lengths`: each row sums to 512; its largest length is exactly 256.
All inputs are finite; a program needn't handle non-finite values.
Results may differ from a plain program's by a relative error of at most 0.014.
Values may be sent and summed in bfloat16 or wider, within the bound.
A program may use at most 64 MiB of HBM per device.

v0:
```python
import math

import jax
import jax.numpy as jnp
from jax import lax
from jax.sharding import PartitionSpec as P


def from_behind(value, axis, by):
    size = lax.axis_size(axis)
    return lax.ppermute(value, axis, [(i, (i + by) % size) for i in range(size)])


def rollout_ids(positions, row_lengths):
    row_ends = jnp.cumsum(row_lengths)
    return jnp.sum((positions[:, None] >= row_ends[None, :]).astype(jnp.int32), axis=1)


def attend(query_shard, pair_shard, row_lengths):
    rows_here = query_shard.shape[1]
    local_heads = pair_shard.shape[2]
    head_dim = pair_shard.shape[3] // 2
    group_size = query_shard.shape[3] // head_dim
    first_pos = lax.axis_index("ctx") * rows_here
    query_pos = first_pos + jnp.arange(rows_here, dtype=jnp.int32)
    query_rollout = rollout_ids(query_pos, row_lengths)
    query_heads = query_shard[0].reshape(rows_here, local_heads, group_size, head_dim)
    score_scale = 1.0 / math.sqrt(head_dim)

    def update(state_in, key_block, key_begin):
        running_max, denom, accum = state_in
        block_len = key_block.shape[0]
        key_pos = key_begin + jnp.arange(block_len, dtype=jnp.int32)
        key_rollout = rollout_ids(key_pos, row_lengths)
        visible = (query_rollout[:, None] == key_rollout[None, :]) & (
            key_pos[None, :] <= query_pos[:, None]
        )
        scores = (
            jnp.einsum(
                "rhgd,khd->hgrk",
                query_heads,
                key_block[:, :, :head_dim],
                preferred_element_type=jnp.float32,
            )
            * score_scale
        )
        scores = jnp.where(visible, scores, -1e30)
        new_max = jnp.maximum(running_max, jnp.max(scores, axis=-1))
        rescale = jnp.exp(running_max - new_max)
        weights = jnp.where(visible, jnp.exp(scores - new_max[..., None]), 0.0)
        denom = denom * rescale + jnp.sum(weights, axis=-1)
        added = jnp.einsum(
            "hgrk,khd->hgrd",
            weights.astype(jnp.bfloat16),
            key_block[:, :, head_dim:],
            preferred_element_type=jnp.float32,
        )
        accum = accum * rescale[..., None] + added
        return (new_max, denom, accum)

    starting = (
        jnp.full((local_heads, group_size, rows_here), -1e30, jnp.float32),
        jnp.zeros((local_heads, group_size, rows_here), jnp.float32),
        jnp.zeros((local_heads, group_size, rows_here, head_dim), jnp.float32),
    )
    shards = lax.all_gather(pair_shard[0], "ctx", axis=0, tiled=True)
    shard_rows = shards.shape[0]
    block_len = math.gcd(shard_rows, 512)

    def one_step(step_index, inner):
        key_block = lax.dynamic_slice_in_dim(shards, step_index * block_len, block_len, 0)
        return update(inner, key_block, step_index * block_len)

    running_max, denom, accum = lax.fori_loop(0, shard_rows // block_len, one_step, starting)
    outputs = accum / denom[..., None]
    outputs = jnp.transpose(outputs, (2, 0, 1, 3)).reshape(
        1, rows_here, local_heads, group_size * head_dim
    )
    return outputs.astype(jnp.bfloat16)


def local(queries, pairs, out_proj, lengths):
    section = lax.axis_index("segment")
    own_result = attend(queries, pairs, lengths[section])
    attended = from_behind(own_result, "segment", -1)
    rows_here = attended.shape[1]
    partial_sum = jnp.dot(
        attended.reshape(rows_here, -1),
        out_proj[0].reshape(-1, out_proj.shape[3]),
        preferred_element_type=jnp.float32,
    )
    shares = lax.psum_scatter(
        partial_sum.astype(jnp.bfloat16), "tp", scatter_dimension=1, tiled=True
    )
    return shares.reshape(1, rows_here, -1)


def solution(mesh):
    return jax.shard_map(
        local,
        mesh=mesh,
        in_specs=(
            P("segment", "ctx", "tp", None),
            P("segment", "ctx", "tp", None),
            P("segment", "tp", None, None),
            P(),
        ),
        out_specs=P("segment", "ctx", "tp"),
        check_vma=False,
    )
```

profile of v0, /device:TPU:21, one launch (start us, length us, event | category | flops | bytes accessed | tf_op | source)
XLA Modules:
  0.0 88.1 jit_solution(15405422814970957084)
XLA Ops:
  6.5 0.0 copy-start
  6.5 0.0 all-gather.3.cloned.1.call-start
  6.5 1.7 %copy.16 = bf16[1,128,4,256]{3,1,2,0:T(8,128)(2,1)} copy(bf16[1,128,4,256]{3,2,1,0:T(4,128)(2,1)} %param.5) | data formatting | bytes 524288 | tf_op args[1]
  8.2 0.0 all-gather.3.cloned.1.call-update
  8.3 0.0 reduce-scatter.2.cloned.1.call-start
  8.3 0.0 copy-done
  8.3 0.2 reduce-window.8
  8.5 1.6 %copy.17 = bf16[1,128,4,640]{1,3,2,0:T(8,128)(2,1)S(1)} copy(bf16[1,128,4,640]{3,2,1,0:T(4,128)(2,1)} %param.4) | data formatting | bytes 1310720 | tf_op args[0]
  10.1 0.1 convert_reduce_fusion
  10.2 0.1 convert_reduce_fusion.1
  10.3 0.1 fusion.24
  10.4 26.1 %all-gather.3.cloned.1.call-done = bf16[1,512,4,256]{3,1,2,0:T(8,128)(2,1)} async-done(((bf16[1,128,4,256]{3,1,2,0:T(8,128)(2,1)}), bf16[1,512,4,256]{3,1,2,0:T(8,128)(2,1)}) %all-gather.3.cloned.1.call-update) | async-done | bytes 1048592 | tf_op jit(solution)/shard_map/all_gather | solution.py:66
  36.6 0.0 copy-start.1
  36.6 2.0 %fusion.8 = (f32[4,5,128]{2,1,0:T(8,128)S(1)}, f32[4,512,128,5]{2,1,3,0:T(8,128)S(1)}) fusion(pred[128,512]{0,1:T(8,128)(4,1)S(1)} %fusion.24, bf16[128,4,5,128]{0,3,2,1:T(8,128)(2,1)S(1)} %bitcast.63, bf16[512,4,256]{2,0,1:T(8,128)(2,1)} %bitcast.65), kind=kOutput, calls=%fused_computation.6 | convolution fusion | flops 339473920 | bytes 6498304 | tf_op jit(solution)/shard_map/while/body/eval_jaxpr/rhgd,khd->hgrk/dot_general | solution.py:39
  38.6 1.3 %fusion.9 = f32[4,5,128]{2,1,0:T(8,128)S(1)} fusion(f32[4,512,128,5]{2,1,3,0:T(8,128)S(1)} %get-tuple-element.26, f32[4,5,128]{2,1,0:T(8,128)S(1)} %get-tuple-element.24, pred[128,512]{0,1:T(8,128)(4,1)S(1)} %fusion.24), kind=kLoop, calls=%fused_computation.7 | loop fusion | flops 6551040 | bytes 5328896 | tf_op jit(solution)/shard_map/while/body/eval_jaxpr/reduce_sum | solution.py:51
  39.9 0.0 copy-done.1
  39.9 1.5 %divide_convert_fusion = bf16[128,4,5,128]{0,3,2,1:T(8,128)(2,1)S(1)} fusion(f32[4,512,128,5]{2,1,3,0:T(8,128)S(1)} %get-tuple-element.26, f32[4,5,128]{2,1,0:T(8,128)S(1)} %get-tuple-element.24, pred[128,512]{0,1:T(8,128)(4,1)S(1)} %fusion.24, f32[128,4,5]{0,2,1:T(8,128)S(1)} %bitcast_add_fusion, f32[128,4,5]{0,2,1:T(8,128)S(1)} %get-tuple-element.23, ...), kind=kOutput, calls=%fused_computation.13 | convolution fusion | flops 343080960 | bytes 6537216 | tf_op jit(solution)/shard_map/while/body/eval_jaxpr/hgrk,khd->hgrd/dot_general | solution.py:52
  41.4 0.3 copy.21
  41.7 0.3 collective-permute-start
  42.0 15.2 %collective-permute-done = bf16[1,128,4,640]{3,1,2,0:T(8,128)(2,1)S(1)} collective-permute-done((bf16[1,128,4,640]{3,1,2,0:T(8,128)(2,1)S(1)}, bf16[1,128,4,640]{3,1,2,0:T(8,128)(2,1)S(1)}, u32[]{:S(2)}, u32[]{:S(2)}) %collective-permute-start) | collective-permute-done | bytes 655392 | tf_op jit(solution)/shard_map/ppermute | solution.py:11
  57.2 11.7 %fusion.5 = bf16[128,5120]{1,0:T(8,128)(2,1)} fusion(bf16[1,4,640,5120]{3,2,1,0:T(8,128)(2,1)} %param.6, bf16[1,128,4,640]{3,1,2,0:T(8,128)(2,1)S(1)} %collective-permute-done), kind=kOutput, calls=%fused_computation.3 | convolution fusion | flops 3356098560 | bytes 28180480 | tf_op jit(solution)/shard_map/dot_general | solution.py:87
  68.9 0.0 reduce-scatter.2.cloned.1.call-update
  69.0 12.3 %reduce-scatter.2.cloned.1.call-done = bf16[128,2560]{1,0:T(8,128)(2,1)} async-done(((bf16[128,5120]{1,0:T(8,128)(2,1)}), bf16[128,2560]{1,0:T(8,128)(2,1)}) %reduce-scatter.2.cloned.1.call-update) | async-done | bytes 655376 | tf_op jit(solution)/shard_map/reduce_scatter | solution.py:92
  (4 shorter events, 0.0 us)
Async XLA Ops:
  6.5 1.8 %copy-start = (s32[4,4]{1,0:T(4,128)S(1)}, s32[4,4]{1,0:T(4,128)}, u32[]{:S(2)}) copy-start(s32[4,4]{1,0:T(4,128)} %param.7) | copy-start | bytes 196
  6.5 30.0 %all-gather.3.cloned.1.call-start = ((), (), s32[]{:S(2)}) async-start(), calls=%async_computation.2 | async-start | bytes 1310720 | tf_op jit(solution)/shard_map/all_gather | solution.py:66
  8.3 73.0 %reduce-scatter.2.cloned.1.call-start = ((), (), s32[]{:S(2)}) async-start(), calls=%async_computation.1 | async-start | bytes 1966080 | tf_op jit(solution)/shard_map/reduce_scatter | solution.py:92
  36.6 3.3 %copy-start.1 = (bf16[1,512,4,256]{3,1,2,0:T(8,128)(2,1)S(1)}, bf16[1,512,4,256]{3,1,2,0:T(8,128)(2,1)}, u32[]{:S(2)}) copy-start(bf16[1,512,4,256]{3,1,2,0:T(8,128)(2,1)} %all-gather.3.cloned.1.call-done) | copy-start | bytes 3145732
  41.7 15.5 %collective-permute-start = (bf16[1,128,4,640]{3,1,2,0:T(8,128)(2,1)S(1)}, bf16[1,128,4,640]{3,1,2,0:T(8,128)(2,1)S(1)}, u32[]{:S(2)}, u32[]{:S(2)}) collective-permute-start(bf16[1,128,4,640]{3,1,2,0:T(8,128)(2,1)S(1)} %copy.21), channel_id=1, source_target_pairs={{0,24},{8,0},{16,8},{24,16},{1,25},{9,1},{17,9},{25,17},{2,26},{10... | collective-permute-start | bytes 1966088 | tf_op jit(solution)/shard_map/ppermute | solution.py:11
Sparse Core Ops, SparseCore 0:
  9.2 27.3 all-gather.2
  69.1 12.1 reduce-scatter.1
where the time goes:
time: 89.3 us; the launch traced here: 88.1 us
  waiting for transfers between devices  53.6 us (60%)
  matrix products  15.2 us (17%)
  between operations  13.5 us (15%)
  local copies, waits for them, and re-layouts  3.62 us (4%)
  other arithmetic  1.76 us (2%)
    all_gather x1, waiting for transfers between devices, attend(): shards = lax.all_gather(pair_shard[0], 'ctx', axis=0, tiled=True)  26.1 us
    ppermute x1, waiting for transfers between devices, from_behind(): lax.ppermute(value, axis, [(i, (i + by) % size) for i in range(size)])  15.2 us
    reduce_scatter x1, waiting for transfers between devices, local(): lax.psum_scatter(partial_sum.astype(jnp.bfloat16), 'tp', scatter_dimensio...  12.3 us
    dot_general x1, matrix products, local(): jnp.dot(attended.reshape(rows_here, -1), out_proj[0].reshape(-1, out_proj...  11.7 us
    unnamed x6, local copies, waits for them, and re-layouts  3.29 us
    dot_general x1, matrix products, update(): jnp.einsum('rhgd,khd->hgrk', query_heads, key_block[:, :, :head_dim], pre...  2.02 us
  transfers between devices with their start and end apart: 3, of which 3 were waited for; matrix products, arithmetic and copies ran while one was open for 2% of the time, Pallas kernels for 0%

commit v1 on v0

v1 whole, which is shorter than its diff:
```python
import functools
import math

import jax
import jax.numpy as jnp
from jax import lax
from jax.experimental import pallas as pl
from jax.experimental.pallas import tpu as pltpu
from jax.sharding import PartitionSpec as P

MESH = pl.DeviceIdType.MESH
HIDDEN = -1e30


def tile_of(columns):
    for tile in (512, 256, 128):
        if columns % tile == 0:
            return tile
    return columns


def kernel(
    sizes,
    lengths_ref,
    q_hbm,
    kv_hbm,
    w_hbm,
    out_ref,
    q_ref,
    kv_ref,
    w_ref,
    seen_ref,
    hide_ref,
    sent_ref,
    got_ref,
    acc_ref,
    part_ref,
    share_ref,
    q_sem,
    kv_sem,
    w_sem,
    seen_send,
    seen_recv,
    att_send,
    att_recv,
    share_send,
    share_recv,
):
    n_seg, n_ctx, n_tp, rows, heads, head_dim, group, back = sizes
    seg = lax.axis_index("segment")
    ctx = lax.axis_index("ctx")
    tp = lax.axis_index("tp")
    width = group * head_dim
    columns = out_ref.shape[1]
    tile = tile_of(columns)
    tiles = columns // tile
    depth = (back + 1) * rows

    kv_copy = pltpu.make_async_copy(kv_hbm, kv_ref, kv_sem)
    kv_copy.start()
    q_copy = pltpu.make_async_copy(q_hbm, q_ref, q_sem)
    q_copy.start()

    def w_copy(h):
        part = pl.ds(pl.multiple_of(h * width, width), width)
        return pltpu.make_async_copy(w_hbm.at[part], w_ref.at[part], w_sem.at[h])

    for h in range(heads):
        w_copy(h).start()

    barrier = pltpu.get_barrier_semaphore()
    greeted = jnp.int32(0)
    for by in range(1, back + 1):
        for peer in (ctx - by, ctx + by):
            valid = (peer >= 0) & (peer < n_ctx)
            greeted = greeted + valid.astype(jnp.int32)

            @pl.when(valid)
            def _():
                pl.semaphore_signal(
                    barrier, inc=1, device_id={"ctx": peer}, device_id_type=MESH
                )

    to_seg = lax.rem(seg + n_seg - 1, n_seg)
    from_seg = lax.rem(seg + 1, n_seg)
    for peer in (to_seg, from_seg):
        pl.semaphore_signal(
            barrier, inc=1, device_id={"segment": peer}, device_id_type=MESH
        )
    for by in range(1, n_tp):
        pl.semaphore_signal(
            barrier,
            inc=1,
            device_id={"tp": lax.rem(tp + by, n_tp)},
            device_id_type=MESH,
        )
    pl.semaphore_wait(barrier, greeted + 2 + n_tp - 1)

    def kv_send(by, h):
        part = pl.ds(pl.multiple_of(h * 2 * head_dim, 2 * head_dim), 2 * head_dim)
        return pltpu.make_async_remote_copy(
            src_ref=kv_ref.at[:, part],
            dst_ref=seen_ref.at[by - 1, :, part],
            send_sem=seen_send.at[by - 1, h],
            recv_sem=seen_recv.at[by - 1, h],
            device_id={"ctx": lax.rem(ctx + by, n_ctx)},
            device_id_type=MESH,
        )

    kv_copy.wait()
    for h in range(heads):
        for by in range(1, back + 1):

            @pl.when(ctx + by < n_ctx)
            def _():
                kv_send(by, h).start()

    for by in range(1, back + 1):

        @pl.when(ctx < by)
        def _():
            seen_ref[by - 1] = jnp.zeros(seen_ref.shape[1:], seen_ref.dtype)

    query_pos = ctx * rows + lax.broadcasted_iota(jnp.int32, (rows, depth), 0)
    key_pos = (ctx - back) * rows + lax.broadcasted_iota(jnp.int32, (rows, depth), 1)
    first = jnp.zeros((rows, depth), jnp.int32)
    end = jnp.int32(0)
    for k in range(lengths_ref.shape[1]):
        end = end + lengths_ref[seg, k]
        first = jnp.where(query_pos >= end, end, first)
    visible = (key_pos >= first) & (key_pos <= query_pos)
    hide_ref[...] = jnp.where(visible, 0.0, HIDDEN)
    acc_ref[...] = jnp.zeros_like(acc_ref)
    q_copy.wait()

    factor = math.log2(math.e) / math.sqrt(head_dim)

    def att_copy(h):
        return pltpu.make_async_remote_copy(
            src_ref=sent_ref.at[h],
            dst_ref=got_ref.at[h],
            send_sem=att_send.at[h],
            recv_sem=att_recv.at[h],
            device_id={"segment": to_seg},
            device_id_type=MESH,
        )

    def attend(h, carry):
        for by in range(1, back + 1):

            @pl.when(ctx >= by)
            def _():
                kv_send(by, h).wait_recv()

        key_part = pl.ds(pl.multiple_of(h * 2 * head_dim, head_dim), head_dim)
        value_part = pl.ds(
            pl.multiple_of(h * 2 * head_dim + head_dim, head_dim), head_dim
        )
        blocks = [seen_ref.at[by - 1] for by in range(back, 0, -1)] + [kv_ref]
        keys = jnp.concatenate([block[:, key_part] for block in blocks], axis=0)
        values = jnp.concatenate([block[:, value_part] for block in blocks], axis=0)
        for g in range(group):
            at = pl.ds(pl.multiple_of((h * group + g) * head_dim, head_dim), head_dim)
            scores = lax.dot_general(
                q_ref[:, at],
                keys,
                (((1,), (1,)), ((), ())),
                preferred_element_type=jnp.float32,
            )
            scores = scores + hide_ref[...]
            peak = jnp.max(scores, axis=1, keepdims=True)
            weights = jnp.exp2((scores - peak) * factor)
            denom = jnp.sum(weights, axis=1, keepdims=True)
            mixed = jnp.dot(
                weights.astype(jnp.bfloat16), values, preferred_element_type=jnp.float32
            )
            sent_ref[h, :, g * head_dim : (g + 1) * head_dim] = (mixed / denom).astype(
                jnp.bfloat16
            )
        att_copy(h).start()
        return carry

    lax.fori_loop(0, heads, attend, 0)

    def w_part(h, begin):
        return w_ref[
            pl.ds(pl.multiple_of(h * width, width), width),
            pl.ds(pl.multiple_of(begin, tile), tile),
        ]

    def total_of(h, begin):
        return acc_ref[:, pl.ds(pl.multiple_of(begin, tile), tile)] + jnp.dot(
            got_ref[h], w_part(h, begin), preferred_element_type=jnp.float32
        )

    def project(h, carry):
        w_copy(h).wait()
        att_copy(h).wait_recv()

        def one(n, inner):
            begin = n * tile
            acc_ref[:, pl.ds(pl.multiple_of(begin, tile), tile)] = total_of(h, begin)
            return inner

        return lax.fori_loop(0, n_tp * tiles, one, carry)

    last = heads - 1
    lax.fori_loop(0, last, project, 0)
    w_copy(last).wait()
    att_copy(last).wait_recv()

    def share_copy(by, n):
        at = pl.ds(pl.multiple_of(n * tile, tile), tile)
        return pltpu.make_async_remote_copy(
            src_ref=part_ref.at[by - 1, :, at],
            dst_ref=share_ref.at[by - 1, :, at],
            send_sem=share_send.at[by - 1, n],
            recv_sem=share_recv.at[by - 1, n],
            device_id={"tp": lax.rem(tp + by, n_tp)},
            device_id_type=MESH,
        )

    for by in range(1, n_tp):
        peer = lax.rem(tp + by, n_tp)

        def theirs(n, inner):
            at = pl.ds(pl.multiple_of(n * tile, tile), tile)
            part_ref[by - 1, :, at] = total_of(last, peer * columns + n * tile).astype(
                jnp.bfloat16
            )
            share_copy(by, n).start()
            return inner

        lax.fori_loop(0, tiles, theirs, 0)

    def ours(n, inner):
        total = total_of(last, tp * columns + n * tile)
        at = pl.ds(pl.multiple_of(n * tile, tile), tile)
        for by in range(1, n_tp):
            share_copy(by, n).wait_recv()
            total = total + share_ref[by - 1, :, at].astype(jnp.float32)
        out_ref[:, at] = total.astype(jnp.bfloat16)
        return inner

    lax.fori_loop(0, tiles, ours, 0)

    for h in range(heads):
        att_copy(h).wait_send()
        for by in range(1, back + 1):

            @pl.when(ctx + by < n_ctx)
            def _():
                kv_send(by, h).wait_send()

    for by in range(1, n_tp):
        for n in range(tiles):
            share_copy(by, n).wait_send()


def local(n_seg, n_ctx, n_tp, queries, pairs, out_proj, lengths):
    rows, heads = pairs.shape[1], pairs.shape[2]
    head_dim = pairs.shape[3] // 2
    width = queries.shape[3]
    group = width // head_dim
    model = out_proj.shape[3]
    columns = model // n_tp
    back = min(n_ctx - 1, -(-(rows * n_ctx // 2 - 1) // rows))
    tiles = columns // tile_of(columns)
    sizes = (n_seg, n_ctx, n_tp, rows, heads, head_dim, group, back)
    bf16 = jnp.bfloat16
    dma = pltpu.SemaphoreType.DMA
    result = pl.pallas_call(
        functools.partial(kernel, sizes),
        out_shape=jax.ShapeDtypeStruct((rows, columns), bf16),
        in_specs=[pl.BlockSpec(memory_space=pltpu.SMEM)]
        + [pl.BlockSpec(memory_space=pl.ANY)] * 3,
        out_specs=pl.BlockSpec(memory_space=pltpu.VMEM),
        scratch_shapes=[
            pltpu.VMEM((rows, heads * width), bf16),
            pltpu.VMEM((rows, heads * 2 * head_dim), bf16),
            pltpu.VMEM((heads * width, model), bf16),
            pltpu.VMEM((back, rows, heads * 2 * head_dim), bf16),
            pltpu.VMEM((rows, (back + 1) * rows), jnp.float32),
            pltpu.VMEM((heads, rows, width), bf16),
            pltpu.VMEM((heads, rows, width), bf16),
            pltpu.VMEM((rows, model), jnp.float32),
            pltpu.VMEM((n_tp - 1, rows, columns), bf16),
            pltpu.VMEM((n_tp - 1, rows, columns), bf16),
            dma,
            dma,
            dma((heads,)),
            dma((back, heads)),
            dma((back, heads)),
            dma((heads,)),
            dma((heads,)),
            dma((n_tp - 1, tiles)),
            dma((n_tp - 1, tiles)),
        ],
        compiler_params=pltpu.CompilerParams(
            collective_id=0, has_side_effects=True, vmem_limit_bytes=60 << 20
        ),
    )(
        lengths,
        queries.reshape(rows, heads * width),
        pairs.reshape(rows, heads * 2 * head_dim),
        out_proj.reshape(heads * width, model),
    )
    return result.reshape(1, rows, columns)


def solution(mesh):
    sizes = [mesh.shape[axis] for axis in ("segment", "ctx", "tp")]
    return jax.shard_map(
        functools.partial(local, *sizes),
        mesh=mesh,
        in_specs=(
            P("segment", "ctx", "tp", None),
            P("segment", "ctx", "tp", None),
            P("segment", "tp", None, None),
            P(),
        ),
        out_specs=P("segment", "ctx", "tp"),
        check_vma=False,
    )
```

time: 89.3 us -> 43.4 us (0.49); the launches traced: 88.1 us -> 43.2 us
  waiting for transfers between devices: 53.6 us -> 0 us
  Pallas kernels: 0 us -> 37.5 us
  matrix products: 15.2 us -> 0 us
  between operations: 13.5 us -> 0.01 us
  local copies, waits for them, and re-layouts: 3.62 us -> 5.64 us
  other arithmetic: 1.76 us -> 0 us
    pallas_call x0 -> x1, Pallas kernels: none -> 37.5 us  [local(): pl.pallas_call(functools.partial(kernel, sizes), out_shape=jax.ShapeDtype...]
    all_gather x1 -> x0, waiting for transfers between devices: 26.1 us -> none  [attend(): shards = lax.all_gather(pair_shard[0], 'ctx', axis=0, tiled=True)]
    dot_general x3 -> x0, matrix products: 15.2 us -> none  [the longest x1 11.7 us: local(): jnp.dot(attended.reshape(rows_here, -1), out_proj[0].reshape(-1, out_proj...]
    ppermute x1 -> x0, waiting for transfers between devices: 15.2 us -> none  [from_behind(): lax.ppermute(value, axis, [(i, (i + by) % size) for i in range(size)])]
    reduce_scatter x1 -> x0, waiting for transfers between devices: 12.3 us -> none  [local(): lax.psum_scatter(partial_sum.astype(jnp.bfloat16), 'tp', scatter_dimensio...]
    unnamed x6 -> x3, local copies, waits for them, and re-layouts: 3.29 us -> 5.64 us
    reduce_sum x3 -> x0, other arithmetic: 1.42 us -> none  [the longest x1 1.25 us: update(): denom = denom * rescale + jnp.sum(weights, axis=-1)]
  transfers between devices with their start and end apart: 3 -> 0, of which waited for: 3 -> 0; matrix products, arithmetic and copies ran while one was open for 2% -> 0% of each run, Pallas kernels for 0% -> 0%
where the time goes in v1:
time: 43.4 us; the launch traced here: 43.2 us
  Pallas kernels  37.5 us (86%)
  local copies, waits for them, and re-layouts  5.64 us (13%)
    pallas_call x1, Pallas kernels, local(): pl.pallas_call(functools.partial(kernel, sizes), out_shape=jax.ShapeDtype...  37.5 us
    unnamed x3, local copies, waits for them, and re-layouts  5.64 us

profile of v1, /device:TPU:21, one launch (start us, length us, event | category | flops | bytes accessed | tf_op | source)
XLA Modules:
  0.0 43.2 jit_solution(7526050791543249461)
XLA Ops:
  0.0 1.7 %copy.6 = bf16[16,8,4,256]{3,1,2,0:T(8,128)(2,1)} copy(bf16[16,8,4,256]{3,2,1,0:T(4,128)(2,1)} %bitcast.13) | data formatting | bytes 524288
  1.7 2.0 %copy.5 = bf16[16,8,4,640]{3,1,2,0:T(8,128)(2,1)} copy(bf16[16,8,4,640]{3,2,1,0:T(4,128)(2,1)} %bitcast.12) | data formatting | bytes 1310720
  3.7 37.5 %shard_map.46 = bf16[128,2560]{1,0:T(8,128)(2,1)} custom-call(s32[4,4]{1,0:T(4,128)} %lengths_ref.1, bf16[128,2560]{1,0:T(8,128)(2,1)} %bitcast.10, bf16[128,1024]{1,0:T(8,128)(2,1)} %bitcast.11, bf16[2560,5120]{1,0:T(8,128)(2,1)} %bitcast.8), custom_call_target="tpu_custom_call" | custom-call | tf_op jit(solution)/shard_map/pallas_call | solution.py:272
  41.2 2.0 %copy.8 = bf16[1,128,2560]{2,1,0:T(8,128)(2,1)} copy(bf16[1,128,2560]{2,1,0:T(8,128)(2,1)} %bitcast.9) | data formatting | bytes 1310720

commit v2 on v1

--- a/solution.py
+++ b/solution.py
@@ -107,11 +107,28 @@
             device_id_type=MESH,
         )
 
+    relayed = n_ctx == 4 and back == 2
+
+    def direct(by):
+        sends = ctx + by < n_ctx
+        return sends & (ctx != 1) if relayed and by == 1 else sends
+
+    def relay(h):
+        part = pl.ds(pl.multiple_of(h * 2 * head_dim, 2 * head_dim), 2 * head_dim)
+        return pltpu.make_async_remote_copy(
+            src_ref=seen_ref.at[1, :, part],
+            dst_ref=seen_ref.at[0, :, part],
+            send_sem=seen_send.at[0, h],
+            recv_sem=seen_recv.at[0, h],
+            device_id={"ctx": 2},
+            device_id_type=MESH,
+        )
+
     kv_copy.wait()
     for h in range(heads):
         for by in range(1, back + 1):
 
-            @pl.when(ctx + by < n_ctx)
+            @pl.when(direct(by))
             def _():
                 kv_send(by, h).start()
 
@@ -146,11 +163,17 @@
         )
 
     def attend(h, carry):
-        for by in range(1, back + 1):
+        for by in range(back, 0, -1):
 
             @pl.when(ctx >= by)
             def _():
                 kv_send(by, h).wait_recv()
+
+            if relayed and by == 2:
+
+                @pl.when(ctx == 3)
+                def _():
+                    relay(h).start()
 
         key_part = pl.ds(pl.multiple_of(h * 2 * head_dim, head_dim), head_dim)
         value_part = pl.ds(
@@ -248,9 +271,15 @@
         att_copy(h).wait_send()
         for by in range(1, back + 1):
 
-            @pl.when(ctx + by < n_ctx)
+            @pl.when(direct(by))
             def _():
                 kv_send(by, h).wait_send()
+
+        if relayed:
+
+            @pl.when(ctx == 3)
+            def _():
+                relay(h).wait_send()
 
     for by in range(1, n_tp):
         for n in range(tiles):
@@ -297,7 +326,7 @@
             dma((n_tp - 1, tiles)),
         ],
         compiler_params=pltpu.CompilerParams(
-            collective_id=0, has_side_effects=True, vmem_limit_bytes=60 << 20
+            collective_id=0, has_side_effects=True, vmem_limit_bytes=40 << 20
         ),
     )(
         lengths,

time: 43.4 us -> 34.8 us (0.80)
  the two profiles are of different devices: /device:TPU:21 before, /device:TPU:29 now
where the time goes in v2:
time: 34.8 us; the launch traced here: 34.6 us
  Pallas kernels  30.9 us (89%)
  local copies, waits for them, and re-layouts  3.66 us (11%)
    pallas_call x1, Pallas kernels, local(): pl.pallas_call(functools.partial(kernel, sizes), out_shape=jax.ShapeDtype...  30.9 us
    unnamed x5, local copies, waits for them, and re-layouts  3.66 us

profile of v2, /device:TPU:29, one launch (start us, length us, event | category | flops | bytes accessed | tf_op | source)
XLA Modules:
  0.0 34.6 jit_solution(15877686013132381076)
XLA Ops:
  0.0 1.0 %copy.6 = bf16[16,8,4,256]{3,1,2,0:T(8,128)(2,1)S(1)} copy(bf16[16,8,4,256]{3,2,1,0:T(4,128)(2,1)} %bitcast.13) | data formatting | bytes 524288
  1.0 1.2 %copy.5 = bf16[16,8,4,640]{3,1,2,0:T(8,128)(2,1)S(1)} copy(bf16[16,8,4,640]{3,2,1,0:T(4,128)(2,1)} %bitcast.12) | data formatting | bytes 1310720
  2.2 0.0 copy-start
  2.2 0.7 %copy-done = s32[4,4]{1,0:T(4,128)S(1)} copy-done((s32[4,4]{1,0:T(4,128)S(1)}, s32[4,4]{1,0:T(4,128)}, u32[]{:S(2)}) %copy-start) | copy-done | bytes 88
  2.8 30.9 %shard_map.46 = bf16[128,2560]{1,0:T(8,128)(2,1)S(1)} custom-call(s32[4,4]{1,0:T(4,128)S(1)} %copy-done, bf16[128,2560]{1,0:T(8,128)(2,1)S(1)} %bitcast.9, bf16[128,1024]{1,0:T(8,128)(2,1)S(1)} %bitcast.10, bf16[2560,5120]{1,0:T(8,128)(2,1)} %bitcast.11), custom_call_target="tpu_custom_call" | custom-call | tf_op jit(solution)/shard_map/pallas_call | solution.py:301
  33.8 0.8 %copy.8 = bf16[1,128,2560]{2,1,0:T(8,128)(2,1)} copy(bf16[1,128,2560]{2,1,0:T(8,128)(2,1)S(1)} %bitcast.8) | data formatting | bytes 1310720
Async XLA Ops:
  2.2 0.7 %copy-start = (s32[4,4]{1,0:T(4,128)S(1)}, s32[4,4]{1,0:T(4,128)}, u32[]{:S(2)}) copy-start(s32[4,4]{1,0:T(4,128)} %lengths_ref.1) | copy-start | bytes 196

commit v3 on v2

--- a/solution.py
+++ b/solution.py
@@ -13,7 +13,7 @@
 
 
 def tile_of(columns):
-    for tile in (512, 256, 128):
+    for tile in (1280, 640, 512, 256, 128):
         if columns % tile == 0:
             return tile
     return columns
@@ -21,13 +21,12 @@
 
 def kernel(
     sizes,
-    lengths_ref,
-    q_hbm,
-    kv_hbm,
+    lengths_hbm,
+    q_ref,
+    kv_ref,
     w_hbm,
     out_ref,
-    q_ref,
-    kv_ref,
+    lengths_ref,
     w_ref,
     seen_ref,
     hide_ref,
@@ -36,8 +35,7 @@
     acc_ref,
     part_ref,
     share_ref,
-    q_sem,
-    kv_sem,
+    lengths_sem,
     w_sem,
     seen_send,
     seen_recv,
@@ -56,10 +54,8 @@
     tiles = columns // tile
     depth = (back + 1) * rows
 
-    kv_copy = pltpu.make_async_copy(kv_hbm, kv_ref, kv_sem)
-    kv_copy.start()
-    q_copy = pltpu.make_async_copy(q_hbm, q_ref, q_sem)
-    q_copy.start()
+    lengths_copy = pltpu.make_async_copy(lengths_hbm, lengths_ref, lengths_sem)
+    lengths_copy.start()
 
     def w_copy(h):
         part = pl.ds(pl.multiple_of(h * width, width), width)
@@ -124,7 +120,6 @@
             device_id_type=MESH,
         )
 
-    kv_copy.wait()
     for h in range(heads):
         for by in range(1, back + 1):
 
@@ -138,6 +133,7 @@
         def _():
             seen_ref[by - 1] = jnp.zeros(seen_ref.shape[1:], seen_ref.dtype)
 
+    lengths_copy.wait()
     query_pos = ctx * rows + lax.broadcasted_iota(jnp.int32, (rows, depth), 0)
     key_pos = (ctx - back) * rows + lax.broadcasted_iota(jnp.int32, (rows, depth), 1)
     first = jnp.zeros((rows, depth), jnp.int32)
@@ -148,16 +144,15 @@
     visible = (key_pos >= first) & (key_pos <= query_pos)
     hide_ref[...] = jnp.where(visible, 0.0, HIDDEN)
     acc_ref[...] = jnp.zeros_like(acc_ref)
-    q_copy.wait()
 
     factor = math.log2(math.e) / math.sqrt(head_dim)
 
-    def att_copy(h):
+    def att_copy(unit):
         return pltpu.make_async_remote_copy(
-            src_ref=sent_ref.at[h],
-            dst_ref=got_ref.at[h],
-            send_sem=att_send.at[h],
-            recv_sem=att_recv.at[h],
+            src_ref=sent_ref.at[unit],
+            dst_ref=got_ref.at[unit],
+            send_sem=att_send.at[unit],
+            recv_sem=att_recv.at[unit],
             device_id={"segment": to_seg},
             device_id_type=MESH,
         )
@@ -197,40 +192,51 @@
             mixed = jnp.dot(
                 weights.astype(jnp.bfloat16), values, preferred_element_type=jnp.float32
             )
-            sent_ref[h, :, g * head_dim : (g + 1) * head_dim] = (mixed / denom).astype(
-                jnp.bfloat16
-            )
-        att_copy(h).start()
+            sent_ref[h * group + g] = (mixed * (1.0 / denom)).astype(jnp.bfloat16)
+            att_copy(h * group + g).start()
         return carry
 
-    lax.fori_loop(0, heads, attend, 0)
-
-    def w_part(h, begin):
-        return w_ref[
-            pl.ds(pl.multiple_of(h * width, width), width),
+    late = max(1, min(group - 1, 2))
+
+    def total_of(h, begin, low, high, tile=tile):
+        mixed = jnp.concatenate(
+            [got_ref[h * group + g] for g in range(low, high)], axis=1
+        )
+        weight = w_ref[
+            pl.ds(
+                pl.multiple_of(h * width + low * head_dim, head_dim),
+                (high - low) * head_dim,
+            ),
             pl.ds(pl.multiple_of(begin, tile), tile),
         ]
-
-    def total_of(h, begin):
         return acc_ref[:, pl.ds(pl.multiple_of(begin, tile), tile)] + jnp.dot(
-            got_ref[h], w_part(h, begin), preferred_element_type=jnp.float32
-        )
-
-    def project(h, carry):
-        w_copy(h).wait()
-        att_copy(h).wait_recv()
+            mixed, weight, preferred_element_type=jnp.float32
+        )
+
+    def project(h, low, high):
+        for g in range(low, high):
+            att_copy(h * group + g).wait_recv()
 
         def one(n, inner):
-            begin = n * tile
-            acc_ref[:, pl.ds(pl.multiple_of(begin, tile), tile)] = total_of(h, begin)
+            begin = pl.multiple_of(n * columns, columns)
+            acc_ref[:, pl.ds(begin, columns)] = total_of(h, begin, low, high, columns)
             return inner
 
-        return lax.fori_loop(0, n_tp * tiles, one, carry)
+        lax.fori_loop(0, n_tp, one, 0)
+
+    def attend_and_project(h, carry):
+        attend(h, 0)
+        w_copy(h - 1).wait()
+        project(h - 1, 0, group)
+        return carry
 
     last = heads - 1
-    lax.fori_loop(0, last, project, 0)
+    attend(0, 0)
+    lax.fori_loop(1, heads, attend_and_project, 0)
     w_copy(last).wait()
-    att_copy(last).wait_recv()
+    project(last, 0, group - late)
+    for g in range(group - late, group):
+        att_copy(last * group + g).wait_recv()
 
     def share_copy(by, n):
         at = pl.ds(pl.multiple_of(n * tile, tile), tile)
@@ -246,29 +252,24 @@
     for by in range(1, n_tp):
         peer = lax.rem(tp + by, n_tp)
 
-        def theirs(n, inner):
+        for n in range(tiles):
             at = pl.ds(pl.multiple_of(n * tile, tile), tile)
-            part_ref[by - 1, :, at] = total_of(last, peer * columns + n * tile).astype(
-                jnp.bfloat16
-            )
+            part_ref[by - 1, :, at] = total_of(
+                last, peer * columns + n * tile, group - late, group
+            ).astype(jnp.bfloat16)
             share_copy(by, n).start()
-            return inner
-
-        lax.fori_loop(0, tiles, theirs, 0)
-
-    def ours(n, inner):
-        total = total_of(last, tp * columns + n * tile)
+
+    for n in range(tiles):
+        total = total_of(last, tp * columns + n * tile, group - late, group)
         at = pl.ds(pl.multiple_of(n * tile, tile), tile)
         for by in range(1, n_tp):
             share_copy(by, n).wait_recv()
             total = total + share_ref[by - 1, :, at].astype(jnp.float32)
         out_ref[:, at] = total.astype(jnp.bfloat16)
-        return inner
-
-    lax.fori_loop(0, tiles, ours, 0)
-
+
+    for unit in range(heads * group):
+        att_copy(unit).wait_send()
     for h in range(heads):
-        att_copy(h).wait_send()
         for by in range(1, back + 1):
 
             @pl.when(direct(by))
@@ -301,27 +302,29 @@
     result = pl.pallas_call(
         functools.partial(kernel, sizes),
         out_shape=jax.ShapeDtypeStruct((rows, columns), bf16),
-        in_specs=[pl.BlockSpec(memory_space=pltpu.SMEM)]
-        + [pl.BlockSpec(memory_space=pl.ANY)] * 3,
+        in_specs=[
+            pl.BlockSpec(memory_space=pltpu.HBM),
+            pl.BlockSpec(memory_space=pltpu.VMEM),
+            pl.BlockSpec(memory_space=pltpu.VMEM),
+            pl.BlockSpec(memory_space=pl.ANY),
+        ],
         out_specs=pl.BlockSpec(memory_space=pltpu.VMEM),
         scratch_shapes=[
-            pltpu.VMEM((rows, heads * width), bf16),
-            pltpu.VMEM((rows, heads * 2 * head_dim), bf16),
+            pltpu.SMEM(lengths.shape, jnp.int32),
             pltpu.VMEM((heads * width, model), bf16),
             pltpu.VMEM((back, rows, heads * 2 * head_dim), bf16),
             pltpu.VMEM((rows, (back + 1) * rows), jnp.float32),
-            pltpu.VMEM((heads, rows, width), bf16),
-            pltpu.VMEM((heads, rows, width), bf16),
+            pltpu.VMEM((heads * group, rows, head_dim), bf16),
+            pltpu.VMEM((heads * group, rows, head_dim), bf16),
             pltpu.VMEM((rows, model), jnp.float32),
             pltpu.VMEM((n_tp - 1, rows, columns), bf16),
             pltpu.VMEM((n_tp - 1, rows, columns), bf16),
             dma,
-            dma,
             dma((heads,)),
             dma((back, heads)),
             dma((back, heads)),
-            dma((heads,)),
-            dma((heads,)),
+            dma((heads * group,)),
+            dma((heads * group,)),
             dma((n_tp - 1, tiles)),
             dma((n_tp - 1, tiles)),
         ],

time: 34.8 us -> 33.7 us (0.968)
  the two profiles are of different devices: /device:TPU:29 before, /device:TPU:21 now
where the time goes in v3:
time: 33.7 us; the launch traced here: 33.5 us
  Pallas kernels  29.8 us (88%)
  local copies, waits for them, and re-layouts  3.66 us (11%)
    pallas_call x1, Pallas kernels, local(): pl.pallas_call(functools.partial(kernel, sizes), out_shape=jax.ShapeDtype...  29.8 us
    unnamed x5, local copies, waits for them, and re-layouts  3.66 us

profile of v3, /device:TPU:21, one launch (start us, length us, event | category | flops | bytes accessed | tf_op | source)
XLA Modules:
  0.0 33.5 jit_solution(7746294904265843704)
XLA Ops:
  0.0 1.0 %copy.6 = bf16[16,8,4,256]{3,1,2,0:T(8,128)(2,1)S(1)} copy(bf16[16,8,4,256]{3,2,1,0:T(4,128)(2,1)} %bitcast.13) | data formatting | bytes 524288
  1.0 1.2 %copy.5 = bf16[16,8,4,640]{3,1,2,0:T(8,128)(2,1)S(1)} copy(bf16[16,8,4,640]{3,2,1,0:T(4,128)(2,1)} %bitcast.12) | data formatting | bytes 1310720
  2.2 0.0 copy-start
  2.2 0.7 %copy-done = s32[4,4]{1,0:T(4,128)S(1)} copy-done((s32[4,4]{1,0:T(4,128)S(1)}, s32[4,4]{1,0:T(4,128)}, u32[]{:S(2)}) %copy-start) | copy-done | bytes 88
  2.8 29.8 %shard_map.46 = bf16[128,2560]{1,0:T(8,128)(2,1)S(1)} custom-call(s32[4,4]{1,0:T(4,128)S(1)} %copy-done, bf16[128,2560]{1,0:T(8,128)(2,1)S(1)} %bitcast.9, bf16[128,1024]{1,0:T(8,128)(2,1)S(1)} %bitcast.10, bf16[2560,5120]{1,0:T(8,128)(2,1)} %bitcast.11), custom_call_target="tpu_custom_call" | custom-call | tf_op jit(solution)/shard_map/pallas_call | solution.py:302
  32.7 0.8 %copy.8 = bf16[1,128,2560]{2,1,0:T(8,128)(2,1)} copy(bf16[1,128,2560]{2,1,0:T(8,128)(2,1)S(1)} %bitcast.8) | data formatting | bytes 1310720
Async XLA Ops:
  2.2 0.7 %copy-start = (s32[4,4]{1,0:T(4,128)S(1)}, s32[4,4]{1,0:T(4,128)}, u32[]{:S(2)}) copy-start(s32[4,4]{1,0:T(4,128)} %lengths_hbm.1) | copy-start | bytes 196

commit v4 on v3

--- a/solution.py
+++ b/solution.py
@@ -103,11 +103,11 @@
             device_id_type=MESH,
         )
 
-    relayed = n_ctx == 4 and back == 2
-
-    def direct(by):
+    relayed = [h for h in range(heads) if h % 2 == 1] if n_ctx == 4 and back == 2 else []
+
+    def direct(by, h):
         sends = ctx + by < n_ctx
-        return sends & (ctx != 1) if relayed and by == 1 else sends
+        return sends & (ctx != 1) if by == 1 and h in relayed else sends
 
     def relay(h):
         part = pl.ds(pl.multiple_of(h * 2 * head_dim, 2 * head_dim), 2 * head_dim)
@@ -123,7 +123,7 @@
     for h in range(heads):
         for by in range(1, back + 1):
 
-            @pl.when(direct(by))
+            @pl.when(direct(by, h))
             def _():
                 kv_send(by, h).start()
 
@@ -157,18 +157,29 @@
             device_id_type=MESH,
         )
 
+    def waits_here(h):
+        here = jnp.bool_(True)
+        for other in relayed:
+            here = here & (h != other)
+        return here
+
+    def pass_on(h):
+        @pl.when(ctx == 3)
+        def _():
+            kv_send(2, h).wait_recv()
+            relay(h).start()
+
     def attend(h, carry):
         for by in range(back, 0, -1):
 
-            @pl.when(ctx >= by)
+            known = ctx >= by
+            if relayed and by == 2:
+                known = known & ((ctx != 3) | waits_here(h))
+
+            @pl.when(known)
             def _():
                 kv_send(by, h).wait_recv()
 
-            if relayed and by == 2:
-
-                @pl.when(ctx == 3)
-                def _():
-                    relay(h).start()
 
         key_part = pl.ds(pl.multiple_of(h * 2 * head_dim, head_dim), head_dim)
         value_part = pl.ds(
@@ -231,7 +242,13 @@
         return carry
 
     last = heads - 1
+    for h in relayed:
+        if h == 0:
+            pass_on(h)
     attend(0, 0)
+    for h in relayed:
+        if h > 0:
+            pass_on(h)
     lax.fori_loop(1, heads, attend_and_project, 0)
     w_copy(last).wait()
     project(last, 0, group - late)
@@ -272,11 +289,11 @@
     for h in range(heads):
         for by in range(1, back + 1):
 
-            @pl.when(direct(by))
+            @pl.when(direct(by, h))
             def _():
                 kv_send(by, h).wait_send()
 
-        if relayed:
+        if h in relayed:
 
             @pl.when(ctx == 3)
             def _():

time: 33.7 us -> 33 us (0.979)
  Pallas kernels: 29.8 us -> 29.1 us
    pallas_call x1, Pallas kernels: 29.8 us -> 29.1 us  [local(): pl.pallas_call(functools.partial(kernel, sizes), out_shape=jax.ShapeDtype...]
where the time goes in v4:
time: 33 us; the launch traced here: 32.8 us
  Pallas kernels  29.1 us (88%)
  local copies, waits for them, and re-layouts  3.66 us (11%)
    pallas_call x1, Pallas kernels, local(): pl.pallas_call(functools.partial(kernel, sizes), out_shape=jax.ShapeDtype...  29.1 us
    unnamed x5, local copies, waits for them, and re-layouts  3.66 us

profile of v4, /device:TPU:21, one launch (start us, length us, event | category | flops | bytes accessed | tf_op | source)
XLA Modules:
  0.0 32.8 jit_solution(16409916640720999523)
XLA Ops:
  0.0 1.0 %copy.6 = bf16[16,8,4,256]{3,1,2,0:T(8,128)(2,1)S(1)} copy(bf16[16,8,4,256]{3,2,1,0:T(4,128)(2,1)} %bitcast.13) | data formatting | bytes 524288
  1.0 1.2 %copy.5 = bf16[16,8,4,640]{3,1,2,0:T(8,128)(2,1)S(1)} copy(bf16[16,8,4,640]{3,2,1,0:T(4,128)(2,1)} %bitcast.12) | data formatting | bytes 1310720
  2.2 0.0 copy-start
  2.2 0.7 %copy-done = s32[4,4]{1,0:T(4,128)S(1)} copy-done((s32[4,4]{1,0:T(4,128)S(1)}, s32[4,4]{1,0:T(4,128)}, u32[]{:S(2)}) %copy-start) | copy-done | bytes 88
  2.8 29.1 %shard_map.46 = bf16[128,2560]{1,0:T(8,128)(2,1)S(1)} custom-call(s32[4,4]{1,0:T(4,128)S(1)} %copy-done, bf16[128,2560]{1,0:T(8,128)(2,1)S(1)} %bitcast.9, bf16[128,1024]{1,0:T(8,128)(2,1)S(1)} %bitcast.10, bf16[2560,5120]{1,0:T(8,128)(2,1)} %bitcast.11), custom_call_target="tpu_custom_call" | custom-call | tf_op jit(solution)/shard_map/pallas_call | solution.py:319
  32.0 0.8 %copy.8 = bf16[1,128,2560]{2,1,0:T(8,128)(2,1)} copy(bf16[1,128,2560]{2,1,0:T(8,128)(2,1)S(1)} %bitcast.8) | data formatting | bytes 1310720
Async XLA Ops:
  2.2 0.7 %copy-start = (s32[4,4]{1,0:T(4,128)S(1)}, s32[4,4]{1,0:T(4,128)}, u32[]{:S(2)}) copy-start(s32[4,4]{1,0:T(4,128)} %lengths_hbm.1) | copy-start | bytes 196

commit v5 on v4

--- a/solution.py
+++ b/solution.py
@@ -207,7 +207,7 @@
             att_copy(h * group + g).start()
         return carry
 
-    late = max(1, min(group - 1, 2))
+    late = group
 
     def total_of(h, begin, low, high, tile=tile):
         mixed = jnp.concatenate(
@@ -251,7 +251,8 @@
             pass_on(h)
     lax.fori_loop(1, heads, attend_and_project, 0)
     w_copy(last).wait()
-    project(last, 0, group - late)
+    if late < group:
+        project(last, 0, group - late)
     for g in range(group - late, group):
         att_copy(last * group + g).wait_recv()
 

time: 33 us -> 33.1 us (level)
  no operation moved by 1% of the time
where the time goes in v5:
time: 33.1 us; the launch traced here: 32.9 us
  Pallas kernels  29.2 us (88%)
  local copies, waits for them, and re-layouts  3.66 us (11%)
    pallas_call x1, Pallas kernels, local(): pl.pallas_call(functools.partial(kernel, sizes), out_shape=jax.ShapeDtype...  29.2 us
    unnamed x5, local copies, waits for them, and re-layouts  3.66 us

profile of v5, /device:TPU:21, one launch (start us, length us, event | category | flops | bytes accessed | tf_op | source)
XLA Modules:
  0.0 32.9 jit_solution(9105028499514337287)
XLA Ops:
  0.0 1.0 %copy.6 = bf16[16,8,4,256]{3,1,2,0:T(8,128)(2,1)S(1)} copy(bf16[16,8,4,256]{3,2,1,0:T(4,128)(2,1)} %bitcast.13) | data formatting | bytes 524288
  1.0 1.2 %copy.5 = bf16[16,8,4,640]{3,1,2,0:T(8,128)(2,1)S(1)} copy(bf16[16,8,4,640]{3,2,1,0:T(4,128)(2,1)} %bitcast.12) | data formatting | bytes 1310720
  2.2 0.0 copy-start
  2.2 0.7 %copy-done = s32[4,4]{1,0:T(4,128)S(1)} copy-done((s32[4,4]{1,0:T(4,128)S(1)}, s32[4,4]{1,0:T(4,128)}, u32[]{:S(2)}) %copy-start) | copy-done | bytes 88
  2.8 29.2 %shard_map.46 = bf16[128,2560]{1,0:T(8,128)(2,1)S(1)} custom-call(s32[4,4]{1,0:T(4,128)S(1)} %copy-done, bf16[128,2560]{1,0:T(8,128)(2,1)S(1)} %bitcast.9, bf16[128,1024]{1,0:T(8,128)(2,1)S(1)} %bitcast.10, bf16[2560,5120]{1,0:T(8,128)(2,1)} %bitcast.11), custom_call_target="tpu_custom_call" | custom-call | tf_op jit(solution)/shard_map/pallas_call | solution.py:320
  32.0 0.8 %copy.8 = bf16[1,128,2560]{2,1,0:T(8,128)(2,1)} copy(bf16[1,128,2560]{2,1,0:T(8,128)(2,1)S(1)} %bitcast.8) | data formatting | bytes 1310720
Async XLA Ops:
  2.2 0.7 %copy-start = (s32[4,4]{1,0:T(4,128)S(1)}, s32[4,4]{1,0:T(4,128)}, u32[]{:S(2)}) copy-start(s32[4,4]{1,0:T(4,128)} %lengths_hbm.1) | copy-start | bytes 196
